TPU v7x, 256 devices: a whole 4x4x8 slice. The times are simulated.
256 devices in a mesh: section: 16 (over x_hi, y, core), tm: 16 (over z, x_lo).
Axes of the slice: x: 4 (x_hi: 2, x_lo: 2; x = x_hi * 2 + x_lo), y: 4, z: 8, core: 2. Of those that a mesh axis runs over, the one named last changes fastest.
Arguments:
- fwd_input: bfloat16 [16, 2048, 1536], P('section', 'tm'), may hold values from -6 to 6
- saved_input: bfloat16 [16, 2048, 1536], P('section', 'tm'), may hold values from -6 to 6
- grad_in: bfloat16 [16, 2048, 1536], P('section', 'tm'), may hold values from -6 to 6
- gain: float32 [16, 1536], P('section'), may hold values from 0.25 to 1.75
- kernel: float32 [16, 31, 1536], P('section'), may hold values from -1 to 1
- w_out: bfloat16 [16, 1536, 1536], P('section', 'tm'), may hold values from -0.15625 to 0.15625
- lengths: int32 [32], replicated, may hold values from 1 to 2048, 49152 in all
- plan: int32 [16, 2], P('section'), may hold values from 0 to 31
Outputs:
- passed_activation: bfloat16 [16, 2048, 1536], P('section', 'tm')
- passed_gradient: bfloat16 [16, 2048, 1536], P('section', 'tm')
- weight_grad: float32 [16, 1536, 1536], P('section', 'tm')
- kernel_grad: float32 [16, 31, 1536], P('section')
- gain_grad: float32 [16, 1536], P('section')
Inputs may be any that keep to these rules, and one draw needn't show every extreme that they name: `lengths`: 32 valid counts summing to 49152, the largest exactly 2048. `plan`: indices into lengths.
All inputs are finite; a program needn't handle non-finite values.
Results may differ from a plain program's by a relative error of at most 0.017.
Values may be sent and summed in bfloat16 or wider, within the bound.
No kernel may reach another device: no remote copies, remote signals or barrier semaphores. Data moves between devices by JAX's collectives and lax.ppermute only.
A program may use at most 64 MiB of HBM per device.

v0:
```python
import jax
import jax.numpy as jnp
from jax import lax
from jax.sharding import PartitionSpec as P

KW = 31


def extended(array, sides, width):
    for axis, dim in sides:
        size, length = (lax.axis_size(axis), array.shape[dim])
        up = [(i, (i + 1) % size) for i in range(size - 1)]
        down = [(j, i) for i, j in up]
        last = lax.slice_in_dim(array, length - width, length, axis=dim)
        first = lax.slice_in_dim(array, 0, width, axis=dim)
        before = lax.ppermute(last, axis, up)
        after = lax.ppermute(first, axis, down)
        array = jnp.concatenate([before, array, after], axis=dim)
    return array


def from_behind(array, axis, by):
    length = lax.axis_size(axis)
    pairs = [(i, i + by) for i in range(length) if 0 <= i + by < length]
    return lax.ppermute(array, axis, pairs)


def normalize(values):
    center = values - jnp.mean(values, axis=-1, keepdims=True)
    inverse = lax.rsqrt(jnp.mean(center * center, axis=-1, keepdims=True) + 1e-05)
    return (center * inverse, inverse)


def swish_act(values):
    return values * jax.nn.sigmoid(values)


def conv_taps(padded, kernel_rows, frames):
    running = jnp.zeros(padded.shape[:-2] + (frames, padded.shape[-1]), jnp.float32)
    for tap_index in range(KW):
        running = running + kernel_rows[tap_index] * padded[..., tap_index : tap_index + frames, :]
    return running


def per_device(fwd_input, saved_input, grad_in, gain, kernel, w_out, lengths, plan):
    frames = fwd_input.shape[1]
    pieces = lax.axis_size("tm")
    margin = KW // 2
    factor = float(frames * pieces) ** (-0.5)
    position = lax.axis_index("tm") * frames + lax.iota(jnp.int32, frames)
    slot_ids = lax.iota(jnp.int32, lengths.shape[0])
    fwd_len = jnp.sum(jnp.where(slot_ids == plan[0, 0], lengths, 0))
    bwd_len = jnp.sum(jnp.where(slot_ids == plan[0, 1], lengths, 0))
    fwd_mask = (position < fwd_len).astype(jnp.float32)[:, None]
    bwd_mask = (position < bwd_len).astype(jnp.float32)[:, None]
    gain_row = gain[0]
    kernel_rows = kernel[0]
    w_rows = w_out[0]
    upstream = grad_in[0]
    fwd_float = fwd_input[0].astype(jnp.float32)
    fwd_hat, unused_inverse = normalize(fwd_float)
    saved_hat, inverse = normalize(saved_input[0].astype(jnp.float32))
    conv_fwd = (fwd_hat * gain_row * fwd_mask).astype(jnp.bfloat16)
    conv_saved = (saved_hat * gain_row * bwd_mask).astype(jnp.bfloat16)
    padded = extended(jnp.stack([conv_fwd, conv_saved]), (("tm", 1),), margin)
    padded_float = padded.astype(jnp.float32)
    mixed_all = conv_taps(padded_float, kernel_rows, frames)
    mixed_saved = mixed_all[1]
    hidden_fwd = swish_act(mixed_all[0]).astype(jnp.bfloat16)
    hidden_saved = swish_act(mixed_saved).astype(jnp.bfloat16)
    columns = hidden_fwd
    product = jnp.dot(
        columns,
        lax.all_gather(w_rows, "tm", axis=0, tiled=True),
        preferred_element_type=jnp.float32,
    )
    hidden_grad = lax.dot_general(
        upstream,
        lax.all_gather(w_rows, "tm", axis=0, tiled=True),
        (((1,), (1,)), ((), ())),
        preferred_element_type=jnp.float32,
    )
    output = (fwd_float + product).astype(jnp.bfloat16)
    passed_activation = from_behind(output[None], "section", 1)
    gate_sig = jax.nn.sigmoid(mixed_saved)
    conv_grad = (hidden_grad * (gate_sig + mixed_saved * gate_sig * (1.0 - gate_sig))).astype(
        jnp.bfloat16
    )
    pad_grad = extended(conv_grad, (("tm", 0),), margin).astype(jnp.float32)
    input_grad = jnp.zeros((frames, conv_grad.shape[1]), jnp.float32)
    for tap_index in range(KW):
        begin_at = 2 * margin - tap_index
        input_grad = input_grad + kernel_rows[tap_index] * pad_grad[begin_at : begin_at + frames]
    grad_float = conv_grad.astype(jnp.float32)
    pad_saved = padded_float[1]
    kernel_local = (
        jnp.stack(
            [
                jnp.sum(grad_float * pad_saved[tap_index : tap_index + frames], axis=0)
                for tap_index in range(KW)
            ]
        )
        * factor
    )
    norm_grad = input_grad * bwd_mask
    gain_local = jnp.sum(norm_grad * saved_hat, axis=0) * factor
    kernel_grad, gain_grad = (
        lax.psum(kernel_local.astype(jnp.bfloat16), "tm").astype(jnp.float32),
        lax.psum(gain_local.astype(jnp.bfloat16), "tm").astype(jnp.float32),
    )
    columns = hidden_saved
    partial_value = (
        lax.dot_general(
            columns, upstream, (((0,), (0,)), ((), ())), preferred_element_type=jnp.float32
        )
        * factor
    )
    weight_grad = lax.psum_scatter(
        lax.optimization_barrier(partial_value.astype(jnp.bfloat16))
        .astype(jnp.float32)
        .astype(jnp.bfloat16),
        "tm",
        scatter_dimension=0,
        tiled=True,
    ).astype(jnp.float32)
    hat_grad = norm_grad * gain_row
    input_back = upstream.astype(jnp.float32) + inverse * (
        hat_grad
        - jnp.mean(hat_grad, axis=-1, keepdims=True)
        - saved_hat * jnp.mean(hat_grad * saved_hat, axis=-1, keepdims=True)
    )
    passed_gradient = from_behind(input_back.astype(jnp.bfloat16)[None], "section", -1)
    return (
        passed_activation,
        passed_gradient,
        weight_grad[None],
        kernel_grad[None],
        gain_grad[None],
    )


def solution(mesh):
    placed = (
        P("section", "tm", None),
        P("section", "tm", None),
        P("section", "tm", None),
        P("section", None),
        P("section", None, None),
        P("section", "tm", None),
        P(),
        P("section", None),
    )
    return jax.shard_map(
        per_device,
        mesh=mesh,
        in_specs=placed,
        out_specs=(
            P("section", "tm", None),
            P("section", "tm", None),
            P("section", "tm", None),
            P("section", None, None),
            P("section", None),
        ),
        check_vma=False,
    )
```

profile of v0, /device:TPU:42, one launch (start us, length us, event | category | flops | bytes accessed | tf_op | source)
XLA Modules:
  0.0 398.9 jit_solution(7578486727265539355)
XLA Ops:
  7.2 0.7 all-gather.3.cloned.1.call-update
  8.0 0.7 reduce.3
  8.7 1.3 fusion.152
  10.0 2.6 fusion.146
  12.6 1.3 compare_convert_fusion
  13.9 1.1 convert_reduce_fusion.1
  15.0 1.1 convert_reduce_fusion
  16.2 1.2 fusion.52
  17.5 0.3 fusion.73
  17.7 0.4 fusion.56
  18.2 3.8 collective-permute-start
  22.0 2.0 collective-permute-start.1
  24.1 0.3 slice_reduce_fusion.30
  24.6 0.2 slice_reduce_fusion.29
  24.9 0.6 collective-permute-done
  25.5 6.0 %collective-permute-done.1 = bf16[2,15,1536]{2,1,0:T(8,128)(2,1)S(1)} collective-permute-done((bf16[2,15,1536]{2,1,0:T(8,128)(2,1)S(1)}, bf16[2,15,1536]{2,1,0:T(8,128)(2,1)S(1)}, u32[]{:S(2)}, u32[]{:S(2)}) %collective-permute-start.1) | collective-permute-done | bytes 92192 | tf_op jit(solution)/shard_map/ppermute | solution.py:17
  31.5 0.3 maximum_convert_fusion
  32.1 6.8 %fusion.20 = f32[2,128,1536]{2,1,0:T(8,128)} fusion(f32[2,158,1536]{2,1,0:T(8,128)S(1)} %maximum_convert_fusion, f32[1536]{0:T(1024)S(1)} %get-tuple-element.68, f32[1536]{0:T(1024)S(1)} %get-tuple-element.69, f32[1536]{0:T(1024)S(1)} %get-tuple-element.40, f32[1536]{0:T(1024)S(1)} %get-tuple-element.41, f32[1536]{0:T(1024)S(1)} %get-tuple-element.42, ...), kind=kLoop, calls=%fused_computation.43 | loop fusion | flops 23986176 | bytes 50522112 | tf_op jit(solution)/shard_map/add | solution.py:41
  38.9 86.8 %all-gather.3.cloned.1.call-done = bf16[1,1536,1536]{2,1,0:T(8,128)(2,1)} async-done(((bf16[1,96,1536]{2,1,0:T(8,128)(2,1)}), bf16[1,1536,1536]{2,1,0:T(8,128)(2,1)}) %all-gather.3.cloned.1.call-update) | async-done | bytes 4718608 | tf_op jit(solution)/shard_map/all_gather | solution.py:74
  125.8 5.5 %fusion.103 = (f32[1536]{0:T(1024)S(1)}, f32[1536]{0:T(1024)S(1)}, f32[1536]{0:T(1024)S(1)}, f32[1536]{0:T(1024)S(1)}, f32[1536]{0:T(1024)S(1)}, /*index=5*/f32[...) fusion(f32[2,158,1536]{2,1,0:T(8,128)S(1)} %maximum_convert_fus, ...), kind=kOutput, calls=%fused_computation.163 | convolution fusion | flops 611037696 | bytes 16594944 | tf_op jit(solution)/shard_map/dot_general | solution.py:77
  131.2 2.0 fusion.104
  133.6 0.6 stack.113
  134.2 0.6 stack.114
  134.8 0.6 stack.115
  135.4 0.6 stack.116
  136.0 0.6 stack.117
  136.6 0.6 stack.118
  137.2 0.6 stack.119
  137.8 1.8 stack.133
  139.6 0.8 broadcast_in_dim.42
  140.4 0.0 reduce-scatter.2.cloned.1.call-start
  140.4 3.6 fusion
  144.1 2.4 collective-permute-start.3
  146.9 3.5 collective-permute-start.4
  150.4 3.9 fusion.17
  154.3 2.1 collective-permute-start.2
  156.4 0.1 maximum_convert_fusion.1
  156.9 5.1 %fusion.72 = (f32[1536]{0:T(1024)S(1)}, f32[128]{0:T(128)S(1)}, f32[128]{0:T(128)S(1)}, f32[128,1536]{1,0:T(8,128)S(1)}) fusion(bf16[1,128,1536]{2,1,0:T(8,128)(2,1)S(1)} %copy-done, f32[128]{0:T(128)S(1)} %copy-done.68, f32[128]{0:T(128)S(1)} %copy-done.66, f32[1536]{0:T(1024)S(1)} %reduce.3, f32[128]{0:T(128)S(1)} %copy-done.70, ...), kind=kLoop, calls=%fused_computation.132 | loop fusion | flops 13957376 | bytes 25764352 | tf_op jit(solution)/shard_map/reduce_sum | solution.py:106
  162.0 0.4 fusion.141
  162.4 3.6 collective-permute-start.5
  166.1 31.3 %psum.15 = bf16[1,1536]{1,0:T(2,128)(2,1)S(1)} all-reduce(bf16[1,1536]{1,0:T(2,128)(2,1)S(1)} %broadcast_in_dim.44), channel_id=1, replica_groups=mesh['section'=16,'tm'=16] {'tm'}, use_global_device_ids=true, to_apply=%region_42.43 | all-reduce | flops 1536 | bytes 6144 | tf_op jit(solution)/shard_map/psum | solution.py:109
  197.4 0.6 broadcast_in_dim.45
  198.0 78.2 %all-reduce.2.cloned.1.call-done = bf16[1,31,1536]{2,0,1:T(2,128)(2,1)} async-done(((bf16[1,31,1536]{2,0,1:T(2,128)(2,1)}), bf16[1,31,1536]{2,0,1:T(2,128)(2,1)}) %all-reduce.2.cloned.1.call-update) | async-done | bytes 95248 | tf_op jit(solution)/shard_map/psum | solution.py:108
  276.2 1.8 broadcast_in_dim.43
  278.0 111.0 %reduce-scatter.2.cloned.1.call-done = bf16[96,1536]{1,0:T(8,128)(2,1)} async-done(((bf16[1536,1536]{1,0:T(8,128)(2,1)}), bf16[96,1536]{1,0:T(8,128)(2,1)}) %reduce-scatter.2.cloned.1.call-update) | async-done | bytes 294928 | tf_op jit(solution)/shard_map/reduce_scatter | solution.py:118
  389.0 1.8 bitcast_convert_fusion
  390.9 0.7 copy.16
  391.6 0.7 copy.17
  (184 shorter events, 0.7 us)
Async XLA Ops:
  7.2 10.6 %copy-start.1 = (bf16[1,128,1536]{2,1,0:T(8,128)(2,1)S(1)}, bf16[1,128,1536]{2,1,0:T(8,128)(2,1)}, u32[]{:S(2)}) copy-start(bf16[1,128,1536]{2,1,0:T(8,128)(2,1)} %param.8) | copy-start | bytes 1179652
  7.2 10.3 %copy-start = (bf16[1,128,1536]{2,1,0:T(8,128)(2,1)S(1)}, bf16[1,128,1536]{2,1,0:T(8,128)(2,1)}, u32[]{:S(2)}) copy-start(bf16[1,128,1536]{2,1,0:T(8,128)(2,1)} %param.9) | copy-start | bytes 1179652
  7.2 118.6 %all-gather.3.cloned.1.call-start = ((), (), s32[]{:S(2)}) async-start(), calls=%async_computation.3 | async-start | bytes 5013504 | tf_op jit(solution)/shard_map/all_gather | solution.py:74
  7.9 268.3 %all-reduce.2.cloned.1.call-start = ((), (), s32[]{:S(2)}) async-start(), calls=%async_computation.2 | async-start | bytes 380928 | tf_op jit(solution)/shard_map/psum | solution.py:108
  17.7 7.8 %copy-start.67 = (f32[128]{0:T(128)}, f32[128]{0:T(128)S(1)}, u32[]{:S(2)}) copy-start(f32[128]{0:T(128)S(1)} %get-tuple-element.84) | copy-start | bytes 1540
  18.2 7.3 %collective-permute-start = (bf16[2,15,1536]{2,1,0:T(8,128)(2,1)S(1)}, bf16[2,15,1536]{2,1,0:T(8,128)(2,1)S(1)}, u32[]{:S(2)}, u32[]{:S(2)}) collective-permute-start(bf16[2,15,1536]{2,1,0:T(8,128)(2,1)S(1)} %get-tuple-element.73), channel_id=1, source_target_pairs={{0,1},{1,2},{2,3},{3,4},{4,5},{5,6},{6,7},{7,8},{8,9},{9,10},{10,1... | collective-permute-start | bytes 276488 | tf_op jit(solution)/shard_map/ppermute | solution.py:16
  22.0 9.5 %collective-permute-start.1 = (bf16[2,15,1536]{2,1,0:T(8,128)(2,1)S(1)}, bf16[2,15,1536]{2,1,0:T(8,128)(2,1)S(1)}, u32[]{:S(2)}, u32[]{:S(2)}) collective-permute-start(bf16[2,15,1536]{2,1,0:T(8,128)(2,1)S(1)} %get-tuple-element.74), channel_id=1, source_target_pairs={{1,0},{2,1},{3,2},{4,3},{5,4},{6,5},{7,6},{8,7},{9,8},{10,9},{11,1... | collective-permute-start | bytes 276488 | tf_op jit(solution)/shard_map/ppermute | solution.py:17
  24.4 7.4 %copy-start.5 = (f32[1536]{0:T(1024)}, f32[1536]{0:T(1024)S(1)}, u32[]{:S(2)}) copy-start(f32[1536]{0:T(1024)S(1)} %get-tuple-element.40) | copy-start | bytes 18436
  24.4 7.4 %copy-start.7 = (f32[1536]{0:T(1024)}, f32[1536]{0:T(1024)S(1)}, u32[]{:S(2)}) copy-start(f32[1536]{0:T(1024)S(1)} %get-tuple-element.41) | copy-start | bytes 18436
  32.1 93.7 %copy-start.3 = (bf16[1,128,1536]{2,1,0:T(8,128)(2,1)S(1)}, bf16[1,128,1536]{2,1,0:T(8,128)(2,1)}, u32[]{:S(2)}) copy-start(bf16[1,128,1536]{2,1,0:T(8,128)(2,1)} %param.10) | copy-start | bytes 1179652
  140.4 248.7 %reduce-scatter.2.cloned.1.call-start = ((), (), s32[]{:S(2)}) async-start(), calls=%async_computation.1 | async-start | bytes 5013504 | tf_op jit(solution)/shard_map/reduce_scatter | solution.py:118
  144.1 12.3 %collective-permute-start.3 = (bf16[15,1536]{1,0:T(8,128)(2,1)S(1)}, bf16[15,1536]{1,0:T(8,128)(2,1)S(1)}, u32[]{:S(2)}, u32[]{:S(2)}) collective-permute-start(bf16[15,1536]{1,0:T(8,128)(2,1)S(1)} %get-tuple-element.75), channel_id=1, source_target_pairs={{0,1},{1,2},{2,3},{3,4},{4,5},{5,6},{6,7},{7,8},{8,9},{9,10},{10,1... | collective-permute-start | bytes 138248 | tf_op jit(solution)/shard_map/ppermute | solution.py:16
  146.5 10.0 %copy-start.6 = (f32[1536]{0:T(1024)S(1)}, f32[1536]{0:T(1024)}, u32[]{:S(2)}) copy-start(f32[1536]{0:T(1024)} %copy-done.5) | copy-start | bytes 18436
  146.5 10.0 %copy-start.8 = (f32[1536]{0:T(1024)S(1)}, f32[1536]{0:T(1024)}, u32[]{:S(2)}) copy-start(f32[1536]{0:T(1024)} %copy-done.7) | copy-start | bytes 18436
  146.6 10.0 %copy-start.10 = (f32[1536]{0:T(1024)S(1)}, f32[1536]{0:T(1024)}, u32[]{:S(2)}) copy-start(f32[1536]{0:T(1024)} %copy-done.9) | copy-start | bytes 18436
  146.6 10.0 %copy-start.12 = (f32[1536]{0:T(1024)S(1)}, f32[1536]{0:T(1024)}, u32[]{:S(2)}) copy-start(f32[1536]{0:T(1024)} %copy-done.11) | copy-start | bytes 18436
  146.6 10.0 %copy-start.14 = (f32[1536]{0:T(1024)S(1)}, f32[1536]{0:T(1024)}, u32[]{:S(2)}) copy-start(f32[1536]{0:T(1024)} %copy-done.13) | copy-start | bytes 18436
  146.6 10.0 %copy-start.16 = (f32[1536]{0:T(1024)S(1)}, f32[1536]{0:T(1024)}, u32[]{:S(2)}) copy-start(f32[1536]{0:T(1024)} %copy-done.15) | copy-start | bytes 18436
  146.6 10.0 %copy-start.18 = (f32[1536]{0:T(1024)S(1)}, f32[1536]{0:T(1024)}, u32[]{:S(2)}) copy-start(f32[1536]{0:T(1024)} %copy-done.17) | copy-start | bytes 18436
  146.6 10.0 %copy-start.20 = (f32[1536]{0:T(1024)S(1)}, f32[1536]{0:T(1024)}, u32[]{:S(2)}) copy-start(f32[1536]{0:T(1024)} %copy-done.19) | copy-start | bytes 18436
  146.6 10.0 %copy-start.22 = (f32[1536]{0:T(1024)S(1)}, f32[1536]{0:T(1024)}, u32[]{:S(2)}) copy-start(f32[1536]{0:T(1024)} %copy-done.21) | copy-start | bytes 18436
  146.6 10.0 %copy-start.24 = (f32[1536]{0:T(1024)S(1)}, f32[1536]{0:T(1024)}, u32[]{:S(2)}) copy-start(f32[1536]{0:T(1024)} %copy-done.23) | copy-start | bytes 18436
  146.6 10.0 %copy-start.26 = (f32[1536]{0:T(1024)S(1)}, f32[1536]{0:T(1024)}, u32[]{:S(2)}) copy-start(f32[1536]{0:T(1024)} %copy-done.25) | copy-start | bytes 18436
  146.6 10.0 %copy-start.28 = (f32[1536]{0:T(1024)S(1)}, f32[1536]{0:T(1024)}, u32[]{:S(2)}) copy-start(f32[1536]{0:T(1024)} %copy-done.27) | copy-start | bytes 18436
  146.7 10.0 %copy-start.30 = (f32[1536]{0:T(1024)S(1)}, f32[1536]{0:T(1024)}, u32[]{:S(2)}) copy-start(f32[1536]{0:T(1024)} %copy-done.29) | copy-start | bytes 18436
  146.7 10.0 %copy-start.32 = (f32[1536]{0:T(1024)S(1)}, f32[1536]{0:T(1024)}, u32[]{:S(2)}) copy-start(f32[1536]{0:T(1024)} %copy-done.31) | copy-start | bytes 18436
  146.7 10.0 %copy-start.34 = (f32[1536]{0:T(1024)S(1)}, f32[1536]{0:T(1024)}, u32[]{:S(2)}) copy-start(f32[1536]{0:T(1024)} %copy-done.33) | copy-start | bytes 18436
  146.7 10.0 %copy-start.36 = (f32[1536]{0:T(1024)S(1)}, f32[1536]{0:T(1024)}, u32[]{:S(2)}) copy-start(f32[1536]{0:T(1024)} %copy-done.35) | copy-start | bytes 18436
  146.7 10.0 %copy-start.38 = (f32[1536]{0:T(1024)S(1)}, f32[1536]{0:T(1024)}, u32[]{:S(2)}) copy-start(f32[1536]{0:T(1024)} %copy-done.37) | copy-start | bytes 18436
  146.7 10.0 %copy-start.40 = (f32[1536]{0:T(1024)S(1)}, f32[1536]{0:T(1024)}, u32[]{:S(2)}) copy-start(f32[1536]{0:T(1024)} %copy-done.39) | copy-start | bytes 18436
  146.7 10.0 %copy-start.42 = (f32[1536]{0:T(1024)S(1)}, f32[1536]{0:T(1024)}, u32[]{:S(2)}) copy-start(f32[1536]{0:T(1024)} %copy-done.41) | copy-start | bytes 18436
  146.7 10.0 %copy-start.44 = (f32[1536]{0:T(1024)S(1)}, f32[1536]{0:T(1024)}, u32[]{:S(2)}) copy-start(f32[1536]{0:T(1024)} %copy-done.43) | copy-start | bytes 18436
  146.7 10.0 %copy-start.46 = (f32[1536]{0:T(1024)S(1)}, f32[1536]{0:T(1024)}, u32[]{:S(2)}) copy-start(f32[1536]{0:T(1024)} %copy-done.45) | copy-start | bytes 18436
  146.7 10.0 %copy-start.48 = (f32[1536]{0:T(1024)S(1)}, f32[1536]{0:T(1024)}, u32[]{:S(2)}) copy-start(f32[1536]{0:T(1024)} %copy-done.47) | copy-start | bytes 18436
  146.8 10.0 %copy-start.50 = (f32[1536]{0:T(1024)S(1)}, f32[1536]{0:T(1024)}, u32[]{:S(2)}) copy-start(f32[1536]{0:T(1024)} %copy-done.49) | copy-start | bytes 18436
  146.8 10.0 %copy-start.52 = (f32[1536]{0:T(1024)S(1)}, f32[1536]{0:T(1024)}, u32[]{:S(2)}) copy-start(f32[1536]{0:T(1024)} %copy-done.51) | copy-start | bytes 18436
  146.8 10.0 %copy-start.54 = (f32[1536]{0:T(1024)S(1)}, f32[1536]{0:T(1024)}, u32[]{:S(2)}) copy-start(f32[1536]{0:T(1024)} %copy-done.53) | copy-start | bytes 18436
  146.8 10.0 %copy-start.56 = (f32[1536]{0:T(1024)S(1)}, f32[1536]{0:T(1024)}, u32[]{:S(2)}) copy-start(f32[1536]{0:T(1024)} %copy-done.55) | copy-start | bytes 18436
  146.8 10.0 %copy-start.58 = (f32[1536]{0:T(1024)S(1)}, f32[1536]{0:T(1024)}, u32[]{:S(2)}) copy-start(f32[1536]{0:T(1024)} %copy-done.57) | copy-start | bytes 18436
  146.8 10.0 %copy-start.60 = (f32[1536]{0:T(1024)S(1)}, f32[1536]{0:T(1024)}, u32[]{:S(2)}) copy-start(f32[1536]{0:T(1024)} %copy-done.59) | copy-start | bytes 18436
  146.8 10.0 %copy-start.62 = (f32[1536]{0:T(1024)S(1)}, f32[1536]{0:T(1024)}, u32[]{:S(2)}) copy-start(f32[1536]{0:T(1024)} %copy-done.61) | copy-start | bytes 18436
  146.8 10.0 %copy-start.64 = (f32[1536]{0:T(1024)S(1)}, f32[1536]{0:T(1024)}, u32[]{:S(2)}) copy-start(f32[1536]{0:T(1024)} %copy-done.63) | copy-start | bytes 18436
  146.8 10.0 %copy-start.66 = (f32[128]{0:T(128)S(1)}, f32[128]{0:T(128)}, u32[]{:S(2)}) copy-start(f32[128]{0:T(128)} %copy-done.65) | copy-start | bytes 1540
  146.8 10.0 %copy-start.68 = (f32[128]{0:T(128)S(1)}, f32[128]{0:T(128)}, u32[]{:S(2)}) copy-start(f32[128]{0:T(128)} %copy-done.67) | copy-start | bytes 1540
  146.9 10.0 %copy-start.70 = (f32[128]{0:T(128)S(1)}, f32[128]{0:T(128)}, u32[]{:S(2)}) copy-start(f32[128]{0:T(128)} %copy-done.69) | copy-start | bytes 1540
  146.9 9.6 %collective-permute-start.4 = (bf16[15,1536]{1,0:T(8,128)(2,1)S(1)}, bf16[15,1536]{1,0:T(8,128)(2,1)S(1)}, u32[]{:S(2)}, u32[]{:S(2)}) collective-permute-start(bf16[15,1536]{1,0:T(8,128)(2,1)S(1)} %get-tuple-element.76), channel_id=1, source_target_pairs={{1,0},{2,1},{3,2},{4,3},{5,4},{6,5},{7,6},{8,7},{9,8},{10,9},{11,1... | collective-permute-start | bytes 138248 | tf_op jit(solution)/shard_map/ppermute | solution.py:17
  154.3 123.7 %collective-permute-start.2 = (bf16[1,128,1536]{2,1,0:T(8,128)(2,1)}, bf16[1,128,1536]{2,1,0:T(8,128)(2,1)S(1)}, u32[]{:S(2)}, u32[]{:S(2)}) collective-permute-start(bf16[1,128,1536]{2,1,0:T(8,128)(2,1)} %fusion.17), channel_id=1, source_target_pairs={{0,16},{16,32},{32,48},{48,64},{64,80},{80,96},{96,112},{112,128},... | collective-permute-start | bytes 1179656 | tf_op jit(solution)/shard_map/ppermute | solution.py:25
  162.4 115.6 %collective-permute-start.5 = (bf16[1,128,1536]{2,1,0:T(8,128)(2,1)S(1)}, bf16[1,128,1536]{2,1,0:T(8,128)(2,1)S(1)}, u32[]{:S(2)}, u32[]{:S(2)}) collective-permute-start(bf16[1,128,1536]{2,1,0:T(8,128)(2,1)S(1)} %fusion.141), channel_id=1, source_target_pairs={{16,0},{32,16},{48,32},{64,48},{80,64},{96,80},{112,96},{128,112},... | collective-permute-start | bytes 1179656 | tf_op jit(solution)/shard_map/ppermute | solution.py:25
  (32 other events, 229.4 us)
Sparse Core Ops, SparseCore 0:
  9.8 115.9 all-gather.2
  140.5 135.6 all-reduce.1
  278.8 110.2 reduce-scatter.1
where the time goes:
time: 400 us; the launch traced here: 399 us
  waiting for transfers between devices  283 us (71%)
  blocking collectives  31.3 us (8%)
  other arithmetic  27.8 us (7%)
  starting transfers between devices  17.7 us (4%)
  between operations  15.3 us (4%)
  matrix products  13 us (3%)
  local copies, waits for them, and re-layouts  10.5 us (3%)
    reduce_scatter x1, waiting for transfers between devices, per_device(): lax.psum_scatter(lax.optimization_barrier(partial_value.astype(jnp.bfloat...  111 us
    all_gather x1, waiting for transfers between devices, per_device(): lax.all_gather(w_rows, 'tm', axis=0, tiled=True)  86.8 us
    psum x1, waiting for transfers between devices, per_device(): lax.psum(kernel_local.astype(jnp.bfloat16), 'tm').astype(jnp.float32)  78.2 us
    psum x1, blocking collectives, per_device(): lax.psum(gain_local.astype(jnp.bfloat16), 'tm').astype(jnp.float32)  31.3 us
  transfers between devices with their start and end apart: 9, of which 5 were waited for; matrix products, arithmetic and copies ran while one was open for 8% of the time, Pallas kernels for 0%

commit v1 on v0

--- a/solution.py
+++ b/solution.py
@@ -4,6 +4,11 @@
 from jax.sharding import PartitionSpec as P
 
 KW = 31
+
+
+def add_all(array, name):
+    parts = lax.all_gather(array, name)
+    return jnp.sum(parts, axis=0)
 
 
 def extended(array, sides, width):
@@ -105,7 +110,7 @@
     norm_grad = input_grad * bwd_mask
     gain_local = jnp.sum(norm_grad * saved_hat, axis=0) * factor
     kernel_grad, gain_grad = (
-        lax.psum(kernel_local.astype(jnp.bfloat16), "tm").astype(jnp.float32),
+        add_all(kernel_local.astype(jnp.bfloat16), "tm").astype(jnp.float32),
         lax.psum(gain_local.astype(jnp.bfloat16), "tm").astype(jnp.float32),
     )
     columns = hidden_saved

time: 400 us -> 329 us (0.82)
  waiting for transfers between devices: 283 us -> 213 us
  local copies, waits for them, and re-layouts: 10.5 us -> 6.16 us
    psum x1 -> x0, waiting for transfers between devices: 78.2 us -> none  [per_device(): lax.psum(kernel_local.astype(jnp.bfloat16), 'tm').astype(jnp.float32)]
    all_gather x0 -> x1, waiting for transfers between devices: none -> 72.8 us  [add_all(): parts = lax.all_gather(array, name)]
    reduce_scatter x1, waiting for transfers between devices: 111 us -> 50.5 us  [per_device(): lax.psum_scatter(lax.optimization_barrier(partial_value.astype(jnp.bfloat...]
    another operation x32, local copies, waits for them, and re-layouts: 6.1 us -> 0.52 us  [per_device(): jnp.stack([jnp.sum(grad_float * pad_saved[tap_index:tap_index + frames],...]
    all_gather x1, waiting for transfers between devices: 86.8 us -> 82.4 us  [per_device(): lax.all_gather(w_rows, 'tm', axis=0, tiled=True)]
  transfers between devices with their start and end apart: 9 -> 9, of which waited for: 5 -> 5; matrix products, arithmetic and copies ran while one was open for 8% -> 13% of each run, Pallas kernels for 0% -> 0%
where the time goes in v1:
time: 329 us; the launch traced here: 327 us
  waiting for transfers between devices  213 us (65%)
  blocking collectives  34.3 us (10%)
  other arithmetic  27.5 us (8%)
  starting transfers between devices  17.5 us (5%)
  between operations  15.3 us (5%)
  matrix products  12.6 us (4%)
  local copies, waits for them, and re-layouts  6.16 us (2%)
    all_gather x1, waiting for transfers between devices, per_device(): lax.all_gather(w_rows, 'tm', axis=0, tiled=True)  82.4 us
    all_gather x1, waiting for transfers between devices, add_all(): parts = lax.all_gather(array, name)  72.8 us
    reduce_scatter x1, waiting for transfers between devices, per_device(): lax.psum_scatter(lax.optimization_barrier(partial_value.astype(jnp.bfloat...  50.5 us
    psum x1, blocking collectives, per_device(): lax.psum(gain_local.astype(jnp.bfloat16), 'tm').astype(jnp.float32)  34.3 us
    ppermute x2, starting transfers between devices, extended(): before = lax.ppermute(last, axis, up)  6.64 us
  transfers between devices with their start and end apart: 9, of which 5 were waited for; matrix products, arithmetic and copies ran while one was open for 13% of the time, Pallas kernels for 0%

profile of v1, /device:TPU:42, one launch (start us, length us, event | category | flops | bytes accessed | tf_op | source)
XLA Modules:
  0.0 326.5 jit_solution(13440001096860377208)
XLA Ops:
  7.2 0.0 all-gather.6.cloned.1.call-start
  7.2 0.7 all-gather.6.cloned.1.call-update
  7.9 0.0 reduce-scatter.2.cloned.1.call-start
  8.0 0.7 reduce.4
  8.7 1.3 fusion.152
  10.0 2.6 fusion.146
  12.6 1.3 compare_convert_fusion
  13.9 1.1 convert_reduce_fusion.1
  15.0 1.1 convert_reduce_fusion
  16.2 1.2 fusion.52
  17.5 0.3 fusion.73
  17.7 0.4 fusion.56
  18.2 0.1 copy-done.67
  18.3 3.8 %collective-permute-start = (bf16[2,15,1536]{2,1,0:T(8,128)(2,1)S(1)}, bf16[2,15,1536]{2,1,0:T(8,128)(2,1)S(1)}, u32[]{:S(2)}, u32[]{:S(2)}) collective-permute-start(bf16[2,15,1536]{2,1,0:T(8,128)(2,1)S(1)} %get-tuple-element.73), channel_id=1, source_target_pairs={{0,1},{1,2},{2,3},{3,4},{4,5},{5,6},{6,7},{7,8},{8,9},{9,10},{10,1... | collective-permute-start | bytes 276488 | tf_op jit(solution)/shard_map/ppermute | solution.py:21
  22.1 2.0 collective-permute-start.1
  24.1 0.3 slice_reduce_fusion.30
  24.6 0.2 slice_reduce_fusion.29
  24.9 0.8 collective-permute-done
  25.7 5.8 %collective-permute-done.1 = bf16[2,15,1536]{2,1,0:T(8,128)(2,1)S(1)} collective-permute-done((bf16[2,15,1536]{2,1,0:T(8,128)(2,1)S(1)}, bf16[2,15,1536]{2,1,0:T(8,128)(2,1)S(1)}, u32[]{:S(2)}, u32[]{:S(2)}) %collective-permute-start.1) | collective-permute-done | bytes 92192 | tf_op jit(solution)/shard_map/ppermute | solution.py:22
  31.6 0.3 maximum_convert_fusion
  32.0 6.0 %fusion.20 = f32[2,128,1536]{2,1,0:T(8,128)S(1)} fusion(f32[2,158,1536]{2,1,0:T(8,128)S(1)} %maximum_convert_fusion, f32[1536]{0:T(1024)S(1)} %get-tuple-element.68, f32[1536]{0:T(1024)S(1)} %get-tuple-element.69, f32[1536]{0:T(1024)S(1)} %get-tuple-element.40, f32[1536]{0:T(1024)S(1)} %get-tuple-element.41, f32[1536]{0:T(1024)S(1)} %get-tuple-element.42, ...), kind=kLoop, calls=%fused_computation.43 | loop fusion | flops 23986176 | bytes 50522112 | tf_op jit(solution)/shard_map/add | solution.py:46
  38.2 1.2 copy-done.2
  39.4 3.6 %fusion = bf16[1536,1536]{1,0:T(8,128)(2,1)} fusion(bf16[1,128,1536]{2,1,0:T(8,128)(2,1)S(1)} %copy-done.3, f32[2,128,1536]{2,1,0:T(8,128)S(1)} %fusion.20), kind=kOutput, calls=%fused_computation.1 | convolution fusion | flops 609681408 | bytes 5898240 | tf_op jit(solution)/shard_map/dot_general | solution.py:118
  42.9 0.0 reduce-scatter.2.cloned.1.call-update
  43.0 0.0 all-gather.4.cloned.1.call-start
  43.0 82.4 %all-gather.6.cloned.1.call-done = bf16[1,1536,1536]{2,1,0:T(8,128)(2,1)} async-done(((bf16[1,96,1536]{2,1,0:T(8,128)(2,1)}), bf16[1,1536,1536]{2,1,0:T(8,128)(2,1)}) %all-gather.6.cloned.1.call-update) | async-done | bytes 4718608 | tf_op jit(solution)/shard_map/all_gather | solution.py:79
  125.4 5.4 %fusion.103 = (f32[1536]{0:T(1024)S(1)}, f32[1536]{0:T(1024)S(1)}, f32[1536]{0:T(1024)S(1)}, f32[1536]{0:T(1024)S(1)}, f32[1536]{0:T(1024)S(1)}, /*index=5*/f32[...) fusion(f32[2,158,1536]{2,1,0:T(8,128)S(1)} %maximum_convert_fus, ...), kind=kOutput, calls=%fused_computation.163 | convolution fusion | flops 611037696 | bytes 16594944 | tf_op jit(solution)/shard_map/dot_general | solution.py:82
  130.9 2.0 fusion.104
  133.4 2.8 collective-permute-start.3
  136.2 3.0 collective-permute-start.4
  139.2 0.3 stack.133
  139.5 3.6 %fusion.17 = bf16[1,128,1536]{2,1,0:T(8,128)(2,1)S(1)} fusion(bf16[1,1536,1536]{2,1,0:T(8,128)(2,1)} %all-gather.6.cloned.1.call-done, bf16[1,128,1536]{2,1,0:T(8,128)(2,1)S(1)} %copy-done.1, f32[2,128,1536]{2,1,0:T(8,128)} %copy-done.2), kind=kOutput, calls=%fused_computation.41 | convolution fusion | flops 605552640 | bytes 6291456 | tf_op jit(solution)/shard_map/dot_general | solution.py:77
  143.5 0.7 multiply_convert_fusion.4
  144.2 2.1 collective-permute-start.2
  146.3 0.0 all-gather.4.cloned.1.call-update
  146.3 0.1 maximum_convert_fusion.1
  146.8 5.1 %fusion.72 = (f32[1536]{0:T(1024)S(1)}, f32[128]{0:T(128)S(1)}, f32[128]{0:T(128)S(1)}, f32[128,1536]{1,0:T(8,128)S(1)}) fusion(bf16[1,128,1536]{2,1,0:T(8,128)(2,1)S(1)} %copy-done, f32[128]{0:T(128)S(1)} %copy-done.68, f32[128]{0:T(128)S(1)} %copy-done.66, f32[1536]{0:T(1024)S(1)} %reduce.4, f32[128]{0:T(128)S(1)} %copy-done.70, ...), kind=kLoop, calls=%fused_computation.132 | loop fusion | flops 13957376 | bytes 25764352 | tf_op jit(solution)/shard_map/reduce_sum | solution.py:111
  151.9 0.4 fusion.141
  152.3 3.6 %collective-permute-start.5 = (bf16[1,128,1536]{2,1,0:T(8,128)(2,1)S(1)}, bf16[1,128,1536]{2,1,0:T(8,128)(2,1)S(1)}, u32[]{:S(2)}, u32[]{:S(2)}) collective-permute-start(bf16[1,128,1536]{2,1,0:T(8,128)(2,1)S(1)} %fusion.141), channel_id=1, source_target_pairs={{16,0},{32,16},{48,32},{64,48},{80,64},{96,80},{112,96},{128,112},... | collective-permute-start | bytes 1179656 | tf_op jit(solution)/shard_map/ppermute | solution.py:30
  156.0 34.3 %psum.7 = bf16[1,1536]{1,0:T(2,128)(2,1)S(1)} all-reduce(bf16[1,1536]{1,0:T(2,128)(2,1)S(1)} %broadcast_in_dim.37), channel_id=1, replica_groups=mesh['section'=16,'tm'=16] {'tm'}, use_global_device_ids=true, to_apply=%region_42.43 | all-reduce | flops 1536 | bytes 6144 | tf_op jit(solution)/shard_map/psum | solution.py:114
  190.3 0.6 broadcast_in_dim.38
  190.9 50.5 %reduce-scatter.2.cloned.1.call-done = bf16[96,1536]{1,0:T(8,128)(2,1)} async-done(((bf16[1536,1536]{1,0:T(8,128)(2,1)}), bf16[96,1536]{1,0:T(8,128)(2,1)}) %reduce-scatter.2.cloned.1.call-update) | async-done | bytes 294928 | tf_op jit(solution)/shard_map/reduce_scatter | solution.py:123
  241.4 1.8 bitcast_convert_fusion
  243.2 72.8 %all-gather.4.cloned.1.call-done = bf16[16,31,1536]{2,1,0:T(8,128)(2,1)} async-done(((bf16[1,31,1536]{2,1,0:T(8,128)(2,1)}), bf16[16,31,1536]{2,1,0:T(8,128)(2,1)}) %all-gather.4.cloned.1.call-update) | async-done | bytes 1523728 | tf_op jit(solution)/shard_map/all_gather | solution.py:10
  316.1 1.7 reduce_sum.411
  317.7 0.8 reshape.683
  318.5 0.7 copy.15
  319.3 0.7 copy.16
  (184 shorter events, 0.6 us)
Async XLA Ops:
  7.2 10.6 %copy-start.1 = (bf16[1,128,1536]{2,1,0:T(8,128)(2,1)S(1)}, bf16[1,128,1536]{2,1,0:T(8,128)(2,1)}, u32[]{:S(2)}) copy-start(bf16[1,128,1536]{2,1,0:T(8,128)(2,1)} %param.8) | copy-start | bytes 1179652
  7.2 10.3 %copy-start = (bf16[1,128,1536]{2,1,0:T(8,128)(2,1)S(1)}, bf16[1,128,1536]{2,1,0:T(8,128)(2,1)}, u32[]{:S(2)}) copy-start(bf16[1,128,1536]{2,1,0:T(8,128)(2,1)} %param.9) | copy-start | bytes 1179652
  7.2 118.2 %all-gather.6.cloned.1.call-start = ((), (), s32[]{:S(2)}) async-start(), calls=%async_computation.3 | async-start | bytes 5013504 | tf_op jit(solution)/shard_map/all_gather | solution.py:79
  7.9 233.5 %reduce-scatter.2.cloned.1.call-start = ((), (), s32[]{:S(2)}) async-start(), calls=%async_computation.1 | async-start | bytes 5013504 | tf_op jit(solution)/shard_map/reduce_scatter | solution.py:123
  13.9 4.3 %copy-start.69 = (f32[128]{0:T(128)}, f32[128]{0:T(128)S(1)}, u32[]{:S(2)}) copy-start(f32[128]{0:T(128)S(1)} %get-tuple-element.82) | copy-start | bytes 1540
  17.4 6.7 %copy-start.4 = (f32[1,31,1536]{2,0,1:T(1,128)S(1)}, f32[1,31,1536]{2,0,1:T(1,128)}, u32[]{:S(2)}) copy-start(f32[1,31,1536]{2,0,1:T(1,128)} %param.12) | copy-start | bytes 571396
  18.3 7.5 %collective-permute-start = (bf16[2,15,1536]{2,1,0:T(8,128)(2,1)S(1)}, bf16[2,15,1536]{2,1,0:T(8,128)(2,1)S(1)}, u32[]{:S(2)}, u32[]{:S(2)}) collective-permute-start(bf16[2,15,1536]{2,1,0:T(8,128)(2,1)S(1)} %get-tuple-element.73), channel_id=1, source_target_pairs={{0,1},{1,2},{2,3},{3,4},{4,5},{5,6},{6,7},{7,8},{8,9},{9,10},{10,1... | collective-permute-start | bytes 276488 | tf_op jit(solution)/shard_map/ppermute | solution.py:21
  22.1 9.5 %collective-permute-start.1 = (bf16[2,15,1536]{2,1,0:T(8,128)(2,1)S(1)}, bf16[2,15,1536]{2,1,0:T(8,128)(2,1)S(1)}, u32[]{:S(2)}, u32[]{:S(2)}) collective-permute-start(bf16[2,15,1536]{2,1,0:T(8,128)(2,1)S(1)} %get-tuple-element.74), channel_id=1, source_target_pairs={{1,0},{2,1},{3,2},{4,3},{5,4},{6,5},{7,6},{8,7},{9,8},{10,9},{11,1... | collective-permute-start | bytes 276488 | tf_op jit(solution)/shard_map/ppermute | solution.py:22
  24.4 7.4 %copy-start.5 = (f32[1536]{0:T(1024)}, f32[1536]{0:T(1024)S(1)}, u32[]{:S(2)}) copy-start(f32[1536]{0:T(1024)S(1)} %get-tuple-element.40) | copy-start | bytes 18436
  24.5 7.4 %copy-start.7 = (f32[1536]{0:T(1024)}, f32[1536]{0:T(1024)S(1)}, u32[]{:S(2)}) copy-start(f32[1536]{0:T(1024)S(1)} %get-tuple-element.41) | copy-start | bytes 18436
  24.5 7.4 %copy-start.9 = (f32[1536]{0:T(1024)}, f32[1536]{0:T(1024)S(1)}, u32[]{:S(2)}) copy-start(f32[1536]{0:T(1024)S(1)} %get-tuple-element.42) | copy-start | bytes 18436
  24.5 7.4 %copy-start.11 = (f32[1536]{0:T(1024)}, f32[1536]{0:T(1024)S(1)}, u32[]{:S(2)}) copy-start(f32[1536]{0:T(1024)S(1)} %get-tuple-element.43) | copy-start | bytes 18436
  24.5 7.4 %copy-start.13 = (f32[1536]{0:T(1024)}, f32[1536]{0:T(1024)S(1)}, u32[]{:S(2)}) copy-start(f32[1536]{0:T(1024)S(1)} %get-tuple-element.44) | copy-start | bytes 18436
  24.5 7.4 %copy-start.15 = (f32[1536]{0:T(1024)}, f32[1536]{0:T(1024)S(1)}, u32[]{:S(2)}) copy-start(f32[1536]{0:T(1024)S(1)} %get-tuple-element.45) | copy-start | bytes 18436
  24.5 7.4 %copy-start.17 = (f32[1536]{0:T(1024)}, f32[1536]{0:T(1024)S(1)}, u32[]{:S(2)}) copy-start(f32[1536]{0:T(1024)S(1)} %get-tuple-element.46) | copy-start | bytes 18436
  24.5 7.4 %copy-start.19 = (f32[1536]{0:T(1024)}, f32[1536]{0:T(1024)S(1)}, u32[]{:S(2)}) copy-start(f32[1536]{0:T(1024)S(1)} %get-tuple-element.47) | copy-start | bytes 18436
  24.5 7.4 %copy-start.21 = (f32[1536]{0:T(1024)}, f32[1536]{0:T(1024)S(1)}, u32[]{:S(2)}) copy-start(f32[1536]{0:T(1024)S(1)} %get-tuple-element.48) | copy-start | bytes 18436
  24.5 7.4 %copy-start.23 = (f32[1536]{0:T(1024)}, f32[1536]{0:T(1024)S(1)}, u32[]{:S(2)}) copy-start(f32[1536]{0:T(1024)S(1)} %get-tuple-element.49) | copy-start | bytes 18436
  24.6 7.4 %copy-start.25 = (f32[1536]{0:T(1024)}, f32[1536]{0:T(1024)S(1)}, u32[]{:S(2)}) copy-start(f32[1536]{0:T(1024)S(1)} %get-tuple-element.50) | copy-start | bytes 18436
  24.6 7.4 %copy-start.27 = (f32[1536]{0:T(1024)}, f32[1536]{0:T(1024)S(1)}, u32[]{:S(2)}) copy-start(f32[1536]{0:T(1024)S(1)} %get-tuple-element.51) | copy-start | bytes 18436
  24.6 7.4 %copy-start.29 = (f32[1536]{0:T(1024)}, f32[1536]{0:T(1024)S(1)}, u32[]{:S(2)}) copy-start(f32[1536]{0:T(1024)S(1)} %get-tuple-element.52) | copy-start | bytes 18436
  24.6 7.4 %copy-start.31 = (f32[1536]{0:T(1024)}, f32[1536]{0:T(1024)S(1)}, u32[]{:S(2)}) copy-start(f32[1536]{0:T(1024)S(1)} %get-tuple-element.53) | copy-start | bytes 18436
  24.6 7.4 %copy-start.33 = (f32[1536]{0:T(1024)}, f32[1536]{0:T(1024)S(1)}, u32[]{:S(2)}) copy-start(f32[1536]{0:T(1024)S(1)} %get-tuple-element.54) | copy-start | bytes 18436
  24.6 7.4 %copy-start.35 = (f32[1536]{0:T(1024)}, f32[1536]{0:T(1024)S(1)}, u32[]{:S(2)}) copy-start(f32[1536]{0:T(1024)S(1)} %get-tuple-element.55) | copy-start | bytes 18436
  24.6 7.4 %copy-start.37 = (f32[1536]{0:T(1024)}, f32[1536]{0:T(1024)S(1)}, u32[]{:S(2)}) copy-start(f32[1536]{0:T(1024)S(1)} %get-tuple-element.56) | copy-start | bytes 18436
  24.6 7.4 %copy-start.39 = (f32[1536]{0:T(1024)}, f32[1536]{0:T(1024)S(1)}, u32[]{:S(2)}) copy-start(f32[1536]{0:T(1024)S(1)} %get-tuple-element.57) | copy-start | bytes 18436
  24.8 13.2 %copy-start.41 = (f32[1536]{0:T(1024)}, f32[1536]{0:T(1024)S(1)}, u32[]{:S(2)}) copy-start(f32[1536]{0:T(1024)S(1)} %get-tuple-element.58) | copy-start | bytes 18436
  24.8 13.2 %copy-start.43 = (f32[1536]{0:T(1024)}, f32[1536]{0:T(1024)S(1)}, u32[]{:S(2)}) copy-start(f32[1536]{0:T(1024)S(1)} %get-tuple-element.59) | copy-start | bytes 18436
  24.8 13.2 %copy-start.45 = (f32[1536]{0:T(1024)}, f32[1536]{0:T(1024)S(1)}, u32[]{:S(2)}) copy-start(f32[1536]{0:T(1024)S(1)} %get-tuple-element.60) | copy-start | bytes 18436
  24.9 13.2 %copy-start.47 = (f32[1536]{0:T(1024)}, f32[1536]{0:T(1024)S(1)}, u32[]{:S(2)}) copy-start(f32[1536]{0:T(1024)S(1)} %get-tuple-element.61) | copy-start | bytes 18436
  24.9 13.2 %copy-start.49 = (f32[1536]{0:T(1024)}, f32[1536]{0:T(1024)S(1)}, u32[]{:S(2)}) copy-start(f32[1536]{0:T(1024)S(1)} %get-tuple-element.62) | copy-start | bytes 18436
  24.9 13.2 %copy-start.51 = (f32[1536]{0:T(1024)}, f32[1536]{0:T(1024)S(1)}, u32[]{:S(2)}) copy-start(f32[1536]{0:T(1024)S(1)} %get-tuple-element.63) | copy-start | bytes 18436
  24.9 13.2 %copy-start.53 = (f32[1536]{0:T(1024)}, f32[1536]{0:T(1024)S(1)}, u32[]{:S(2)}) copy-start(f32[1536]{0:T(1024)S(1)} %get-tuple-element.64) | copy-start | bytes 18436
  24.9 13.2 %copy-start.55 = (f32[1536]{0:T(1024)}, f32[1536]{0:T(1024)S(1)}, u32[]{:S(2)}) copy-start(f32[1536]{0:T(1024)S(1)} %get-tuple-element.65) | copy-start | bytes 18436
  24.9 13.2 %copy-start.57 = (f32[1536]{0:T(1024)}, f32[1536]{0:T(1024)S(1)}, u32[]{:S(2)}) copy-start(f32[1536]{0:T(1024)S(1)} %get-tuple-element.66) | copy-start | bytes 18436
  24.9 13.2 %copy-start.59 = (f32[1536]{0:T(1024)}, f32[1536]{0:T(1024)S(1)}, u32[]{:S(2)}) copy-start(f32[1536]{0:T(1024)S(1)} %get-tuple-element.67) | copy-start | bytes 18436
  24.9 13.2 %copy-start.61 = (f32[1536]{0:T(1024)}, f32[1536]{0:T(1024)S(1)}, u32[]{:S(2)}) copy-start(f32[1536]{0:T(1024)S(1)} %get-tuple-element.68) | copy-start | bytes 18436
  24.9 13.2 %copy-start.63 = (f32[1536]{0:T(1024)}, f32[1536]{0:T(1024)S(1)}, u32[]{:S(2)}) copy-start(f32[1536]{0:T(1024)S(1)} %get-tuple-element.69) | copy-start | bytes 18436
  32.0 7.3 %copy-start.3 = (bf16[1,128,1536]{2,1,0:T(8,128)(2,1)S(1)}, bf16[1,128,1536]{2,1,0:T(8,128)(2,1)}, u32[]{:S(2)}) copy-start(bf16[1,128,1536]{2,1,0:T(8,128)(2,1)} %param.10) | copy-start | bytes 1179652
  43.0 273.1 %all-gather.4.cloned.1.call-start = ((), (), s32[]{:S(2)}) async-start(), calls=%async_computation.2 | async-start | bytes 1671168 | tf_op jit(solution)/shard_map/all_gather | solution.py:10
  133.4 12.9 %collective-permute-start.3 = (bf16[15,1536]{1,0:T(8,128)(2,1)S(1)}, bf16[15,1536]{1,0:T(8,128)(2,1)S(1)}, u32[]{:S(2)}, u32[]{:S(2)}) collective-permute-start(bf16[15,1536]{1,0:T(8,128)(2,1)S(1)} %get-tuple-element.75), channel_id=1, source_target_pairs={{0,1},{1,2},{2,3},{3,4},{4,5},{5,6},{6,7},{7,8},{8,9},{9,10},{10,1... | collective-permute-start | bytes 138248 | tf_op jit(solution)/shard_map/ppermute | solution.py:21
  136.2 10.1 %collective-permute-start.4 = (bf16[15,1536]{1,0:T(8,128)(2,1)S(1)}, bf16[15,1536]{1,0:T(8,128)(2,1)S(1)}, u32[]{:S(2)}, u32[]{:S(2)}) collective-permute-start(bf16[15,1536]{1,0:T(8,128)(2,1)S(1)} %get-tuple-element.76), channel_id=1, source_target_pairs={{1,0},{2,1},{3,2},{4,3},{5,4},{6,5},{7,6},{8,7},{9,8},{10,9},{11,1... | collective-permute-start | bytes 138248 | tf_op jit(solution)/shard_map/ppermute | solution.py:22
  143.2 3.3 %copy-start.6 = (f32[1536]{0:T(1024)S(1)}, f32[1536]{0:T(1024)}, u32[]{:S(2)}) copy-start(f32[1536]{0:T(1024)} %copy-done.5) | copy-start | bytes 18436
  143.2 3.3 %copy-start.8 = (f32[1536]{0:T(1024)S(1)}, f32[1536]{0:T(1024)}, u32[]{:S(2)}) copy-start(f32[1536]{0:T(1024)} %copy-done.7) | copy-start | bytes 18436
  143.2 3.3 %copy-start.10 = (f32[1536]{0:T(1024)S(1)}, f32[1536]{0:T(1024)}, u32[]{:S(2)}) copy-start(f32[1536]{0:T(1024)} %copy-done.9) | copy-start | bytes 18436
  143.2 3.3 %copy-start.12 = (f32[1536]{0:T(1024)S(1)}, f32[1536]{0:T(1024)}, u32[]{:S(2)}) copy-start(f32[1536]{0:T(1024)} %copy-done.11) | copy-start | bytes 18436
  144.2 46.7 %collective-permute-start.2 = (bf16[1,128,1536]{2,1,0:T(8,128)(2,1)S(1)}, bf16[1,128,1536]{2,1,0:T(8,128)(2,1)S(1)}, u32[]{:S(2)}, u32[]{:S(2)}) collective-permute-start(bf16[1,128,1536]{2,1,0:T(8,128)(2,1)S(1)} %fusion.17), channel_id=1, source_target_pairs={{0,16},{16,32},{32,48},{48,64},{64,80},{80,96},{96,112},{112,128},... | collective-permute-start | bytes 1179656 | tf_op jit(solution)/shard_map/ppermute | solution.py:30
  152.3 38.6 %collective-permute-start.5 = (bf16[1,128,1536]{2,1,0:T(8,128)(2,1)S(1)}, bf16[1,128,1536]{2,1,0:T(8,128)(2,1)S(1)}, u32[]{:S(2)}, u32[]{:S(2)}) collective-permute-start(bf16[1,128,1536]{2,1,0:T(8,128)(2,1)S(1)} %fusion.141), channel_id=1, source_target_pairs={{16,0},{32,16},{48,32},{64,48},{80,64},{96,80},{112,96},{128,112},... | collective-permute-start | bytes 1179656 | tf_op jit(solution)/shard_map/ppermute | solution.py:30
  (32 other events, 97.3 us)
Sparse Core Ops, SparseCore 0:
  9.8 115.5 all-gather.5
  128.0 113.3 reduce-scatter.1
  243.8 72.2 all-gather.3
